TPU v7x, 1024 devices: a whole 4x8x16 slice. The times are simulated.
1024 devices in a mesh: row: 128 (over x, y_hi, z), col: 8 (over y_lo, core).
Axes of the slice: x: 4, y: 8 (y_hi: 2, y_lo: 4; y = y_hi * 4 + y_lo), z: 16, core: 2. Of those that a mesh axis runs over, the one named last changes fastest.
Arguments:
- tokens: bfloat16 [256, 8192], P('row', 'col'), may hold values from -6 to 6
- out_grad: bfloat16 [256, 8192], P('row', 'col'), may hold values from -1.5 to 1.5
- in_weight: bfloat16 [128, 8, 128, 128], P('row', 'col'), may hold values from -0.1875 to 0.1875
- out_weight: bfloat16 [128, 8, 128, 128], P('row', 'col'), may hold values from -0.125 to 0.125
- in_blocks: int32 [128, 8], P(None, 'col'), may hold values from 0 to 63, as said below
- out_blocks: int32 [128, 8], P(None, 'col'), may hold values from 0 to 63, as said below
Outputs:
- mixed: bfloat16 [256, 8192], P('row', 'col')
- in_grad: bfloat16 [256, 8192], P('row', 'col')
- in_weight_grad: float32 [128, 8, 128, 128], P('row', 'col')
- out_weight_grad: float32 [128, 8, 128, 128], P('row', 'col')
Inputs may be any that keep to these rules, and one draw needn't show every extreme that they name: `in_blocks`: each row j names 8 distinct feature blocks, 1 in each run of 8 blocks, runs in order along the row (entries k * 1 to (k + 1) - 1 lie in blocks k * 8 to (k + 1) * 8 - 1); inside a run the block's offset differs from j mod 8 in at most one bit. `out_blocks`: same structure as in_blocks, drawn independently.
All inputs are finite; a program needn't handle non-finite values.
Results may differ from a plain program's by a relative error of at most 0.0049.
Values may be sent and summed in bfloat16 or wider, within the bound.
No kernel may reach another device: no remote copies, remote signals or barrier semaphores. Data moves between devices by JAX's collectives and lax.ppermute only.
A program may use at most 32 MiB of HBM per device.

v0:
```python
import math

import jax
import jax.numpy as jnp
from jax import lax
from jax.sharding import PartitionSpec as P


def gelu_slope(value):
    cdf = 0.5 * (1.0 + jax.scipy.special.erf(value * 2.0 ** (-0.5)))
    pdf = jnp.exp(-0.5 * value * value) * (2.0 * math.pi) ** (-0.5)
    return cdf + value * pdf


def place_blocks(terms, offsets, slots):
    table = (offsets[:, :, None] == jnp.arange(slots, dtype=jnp.int32)[None, None, :]).astype(
        jnp.float32
    )
    placed = jnp.einsum("thpb,hps->tsb", terms, table, precision=lax.Precision.HIGHEST)
    return placed.reshape(terms.shape[0], slots * terms.shape[3])


def body(tokens, out_grad, in_weight, out_weight, in_blocks, out_blocks):
    row_count = lax.axis_size("row")
    hid = in_weight.shape[0]
    width = in_weight.shape[2]
    slots = tokens.shape[1] // width
    local_rows = tokens.shape[0]
    total = local_rows * row_count
    first = lax.axis_index("row") * hid
    every_in = in_blocks % slots
    every_out = out_blocks % slots
    own_in = lax.dynamic_slice_in_dim(every_in, first, hid, 0)
    own_out = lax.dynamic_slice_in_dim(every_out, first, hid, 0)
    every_x, every_dy = (
        lax.all_gather(tokens, "row", axis=0, tiled=True),
        lax.all_gather(out_grad, "row", axis=0, tiled=True),
    )
    picked_x = every_x.reshape(total, slots, width)[:, own_in]
    picked_dy = every_dy.reshape(total, slots, width)[:, own_out]
    partial_value = jnp.einsum(
        "thpb,hpbo->tho", picked_x, in_weight, preferred_element_type=jnp.float32
    )
    hidden = lax.psum(partial_value, "col")
    active = jax.nn.gelu(hidden, approximate=False).astype(jnp.bfloat16)
    back_part = jnp.einsum(
        "thpo,hpio->thi", picked_dy, out_weight, preferred_element_type=jnp.float32
    )
    hidden_grad = lax.psum(back_part, "col")
    pre_grad = (hidden_grad * gelu_slope(hidden)).astype(jnp.bfloat16)
    part = active
    terms = jnp.einsum("thi,hpio->thpo", part, out_weight, preferred_element_type=jnp.float32)
    mixed = lax.psum_scatter(
        place_blocks(terms, own_out, slots), "row", scatter_dimension=0, tiled=True
    ).astype(jnp.bfloat16)
    part = pre_grad
    terms = jnp.einsum("tho,hpbo->thpb", part, in_weight, preferred_element_type=jnp.float32)
    in_grad = lax.psum_scatter(
        place_blocks(terms, own_in, slots), "row", scatter_dimension=0, tiled=True
    ).astype(jnp.bfloat16)
    out_weight_grad = jnp.einsum(
        "thi,thpo->hpio", active, picked_dy, preferred_element_type=jnp.float32
    )
    in_weight_grad = jnp.einsum(
        "thpb,tho->hpbo", picked_x, pre_grad, preferred_element_type=jnp.float32
    )
    return (mixed, in_grad, in_weight_grad, out_weight_grad)


def solution(mesh):
    placed = (
        P("row", "col"),
        P("row", "col"),
        P("row", "col", None, None),
        P("row", "col", None, None),
        P(None, "col"),
        P(None, "col"),
    )
    return jax.shard_map(
        body,
        mesh=mesh,
        in_specs=placed,
        out_specs=(
            P("row", "col"),
            P("row", "col"),
            P("row", "col", None, None),
            P("row", "col", None, None),
        ),
        check_vma=False,
    )
```

profile of v0, /device:TPU:8, one launch (start us, length us, event | category | flops | bytes accessed | tf_op | source)
XLA Modules:
  0.0 1860.2 jit_solution(1081484668236514778)
XLA Ops:
  7.2 0.0 copy-start
  7.2 0.0 all-reduce.7.cloned.1.call-start
  7.2 0.0 copy-start.4
  7.2 0.6 copy-done.4
  7.9 0.0 copy-start.5
  7.9 0.6 copy-done.5
  8.6 0.6 fusion.38
  9.1 0.0 copy-start.2
  10.5 0.0 copy-done.2
  10.5 449.9 %all-gather = bf16[128,2,1024]{2,1,0:T(2,128)(2,1)S(1)} all-gather(bf16[1,2,1024]{2,1,0:T(2,128)(2,1)S(1)} %bitcast.87), channel_id=1, replica_groups=mesh['row'=128,'col'=8] {'row'}, dimensions={0}, use_global_device_ids=true | all-gather | bytes 528384 | tf_op jit(solution)/shard_map/all_gather | solution.py:36
  460.4 0.0 copy-start.3
  460.4 0.3 reshape.105
  460.7 0.3 copy-done.3
  461.0 428.5 %all-gather.1 = bf16[128,2,1024]{2,1,0:T(2,128)(2,1)S(1)} all-gather(bf16[1,2,1024]{2,1,0:T(2,128)(2,1)S(1)} %bitcast.88), channel_id=1, replica_groups=mesh['row'=128,'col'=8] {'row'}, dimensions={0}, use_global_device_ids=true | all-gather | bytes 528384 | tf_op jit(solution)/shard_map/all_gather | solution.py:37
  889.6 0.3 reshape.113
  892.5 0.1 constant_dynamic-slice_fusion.1
  892.7 0.0 copy-done
  892.7 0.8 convolution_bitcast_fusion.1
  893.5 0.0 copy-start.1
  893.5 0.1 constant_dynamic-slice_fusion
  893.6 0.6 copy-done.1
  894.2 0.8 convolution_bitcast_fusion
  895.0 0.0 all-reduce.7.cloned.1.call-update
  895.1 1.3 dynamic-slice.8
  897.0 0.7 fusion.35
  897.7 0.7 fusion.34
  898.3 66.6 %all-reduce.7.cloned.1.call-done = (f32[256,1,128]{2,0,1:T(8,128)}, f32[256,1,128]{2,0,1:T(8,128)}) async-done(((f32[256,1,128]{2,0,1:T(8,128)}, f32[256,1,128]{2,0,1:T(8,128)}), (f32[256,1,128]{2,0,1:T(8,128)}, f32[256,1,128]{2,0,1:T(8,128)})) %all-reduce.7.cloned.1.call-update) | async-done | bytes 262160 | tf_op jit(solution)/shard_map/psum | solution.py:44
  964.9 1.3 fusion.8
  966.3 0.8 convolution_bitcast_fusion.3
  967.1 0.2 fusion.21
  967.3 0.2 convolution_bitcast_fusion.2
  967.5 0.1 fusion.24
  967.6 0.7 copy.13
  968.3 0.1 broadcast_multiply_fusion.1
  968.5 0.2 copy.37
  968.7 0.1 broadcast_multiply_fusion
  968.8 0.2 copy.36
  969.0 883.1 %all-reduce.8 = (bf16[256,1024]{1,0:T(8,128)(2,1)S(1)}, bf16[256,1024]{1,0:T(8,128)(2,1)S(1)}) all-reduce(f32[256,1024]{1,0:T(8,128)S(1)} %bitcast.83, f32[256,1024]{1,0:T(8,128)S(1)} %bitcast.84), channel_id=2, replica_groups=mesh['row'=128,'col'=8] {'row'}, use_global_device_ids=true, to_apply=%region_1.2.clone | all-reduce | flops 524288 | bytes 3145728
  1852.1 0.6 dynamic-slice_convert_fusion.1
  1852.7 0.6 dynamic-slice_convert_fusion
  (2 shorter events, 0.0 us)
Async XLA Ops:
  7.2 885.5 %copy-start = (bf16[1,1,128,128]{3,2,1,0:T(8,128)(2,1)S(1)}, bf16[1,1,128,128]{3,2,1,0:T(8,128)(2,1)}, u32[]{:S(2)}) copy-start(bf16[1,1,128,128]{3,2,1,0:T(8,128)(2,1)} %param.8) | copy-start | bytes 98308
  7.2 957.8 %all-reduce.7.cloned.1.call-start = ((), (), s32[]{:S(2)}) async-start(), calls=%async_computation | async-start | bytes 524288 | tf_op jit(solution)/shard_map/psum | solution.py:44
  7.2 0.7 copy-start.4
  7.9 0.7 copy-start.5
  9.1 1.3 copy-start.2
  460.4 0.7 copy-start.3
  893.5 0.8 copy-start.1
Sparse Core Ops, SparseCore 0:
  895.2 69.7 all-reduce.6
where the time goes:
time: 1860 us
  blocking collectives  1760 us (95%)
  waiting for transfers between devices  66.6 us (4%)
  between operations  18.7 us (1%)
    unnamed x1, blocking collectives  883 us
    all_gather x1, blocking collectives, body(): lax.all_gather(tokens, 'row', axis=0, tiled=True)  450 us
    all_gather x1, blocking collectives, body(): lax.all_gather(out_grad, 'row', axis=0, tiled=True)  429 us
    psum x1, waiting for transfers between devices, body(): hidden = lax.psum(partial_value, 'col')  66.6 us
  transfers between devices with their start and end apart: 1, of which 1 were waited for; matrix products, arithmetic and copies ran while one was open for 0% of the time, Pallas kernels for 0%

commit v1 on v0

v1 whole, which is shorter than its diff:
```python
import math

import jax
import jax.numpy as jnp
from jax import lax
from jax.sharding import PartitionSpec as P


def gelu_slope(value):
    cdf = 0.5 * (1.0 + jax.scipy.special.erf(value * 2.0 ** (-0.5)))
    pdf = jnp.exp(-0.5 * value * value) * (2.0 * math.pi) ** (-0.5)
    return cdf + value * pdf


def body(tokens, out_grad, in_weight, out_weight, in_blocks, out_blocks):
    row_count = lax.axis_size("row")
    width = in_weight.shape[2]
    slots = tokens.shape[1] // width
    local_rows = tokens.shape[0]
    total = local_rows * row_count
    every_in = in_blocks[:, 0] % slots
    every_out = out_blocks[:, 0] % slots
    w_in = in_weight[0, 0]
    w_out = out_weight[0, 0]
    x3 = tokens.reshape(local_rows, slots, width)
    dy3 = out_grad.reshape(local_rows, slots, width)
    send = jnp.stack([x3[:, every_in], dy3[:, every_out]], axis=0)
    send = send.transpose(2, 0, 1, 3).reshape(row_count * 2 * local_rows, width)
    got = lax.all_to_all(send, "row", 0, 0, tiled=True)
    got = got.reshape(row_count, 2, local_rows, width)
    picked_x = got[:, 0].reshape(total, width)
    picked_dy = got[:, 1].reshape(total, width)
    parts = jnp.stack(
        [
            jnp.dot(picked_x, w_in, preferred_element_type=jnp.float32),
            lax.dot_general(
                picked_dy, w_out, (((1,), (1,)), ((), ())), preferred_element_type=jnp.float32
            ),
        ],
        axis=0,
    )
    sums = lax.psum(parts, "col")
    hidden = sums[0]
    hidden_grad = sums[1]
    active = jax.nn.gelu(hidden, approximate=False).astype(jnp.bfloat16)
    pre_grad = (hidden_grad * gelu_slope(hidden)).astype(jnp.bfloat16)
    mixed_terms = jnp.dot(active, w_out, preferred_element_type=jnp.float32)
    in_terms = lax.dot_general(
        pre_grad, w_in, (((1,), (1,)), ((), ())), preferred_element_type=jnp.float32
    )
    back = jnp.stack([mixed_terms, in_terms], axis=1).reshape(total * 2, width)
    back = lax.all_to_all(back, "row", 0, 0, tiled=True)
    back = back.reshape(row_count, local_rows, 2, width)
    slot_ids = jnp.arange(slots, dtype=jnp.int32)
    out_table = (every_out[:, None] == slot_ids[None, :]).astype(jnp.float32)
    in_table = (every_in[:, None] == slot_ids[None, :]).astype(jnp.float32)
    mixed = jnp.einsum(
        "jb,jtf->tbf", out_table, back[:, :, 0], precision=lax.Precision.HIGHEST
    ).reshape(local_rows, slots * width)
    in_grad = jnp.einsum(
        "jb,jtf->tbf", in_table, back[:, :, 1], precision=lax.Precision.HIGHEST
    ).reshape(local_rows, slots * width)
    out_weight_grad = lax.dot_general(
        active, picked_dy, (((0,), (0,)), ((), ())), preferred_element_type=jnp.float32
    )
    in_weight_grad = lax.dot_general(
        picked_x, pre_grad, (((0,), (0,)), ((), ())), preferred_element_type=jnp.float32
    )
    return (
        mixed.astype(jnp.bfloat16),
        in_grad.astype(jnp.bfloat16),
        in_weight_grad[None, None],
        out_weight_grad[None, None],
    )


def solution(mesh):
    placed = (
        P("row", "col"),
        P("row", "col"),
        P("row", "col", None, None),
        P("row", "col", None, None),
        P(None, "col"),
        P(None, "col"),
    )
    return jax.shard_map(
        body,
        mesh=mesh,
        in_specs=placed,
        out_specs=(
            P("row", "col"),
            P("row", "col"),
            P("row", "col", None, None),
            P("row", "col", None, None),
        ),
        check_vma=False,
    )
```

time: 1860 us -> 191 us (0.10)
  the two profiles are of different devices: /device:TPU:8 before, /device:TPU:2 now
where the time goes in v1:
time: 191 us
  waiting for transfers between devices  96.5 us (51%)
  blocking collectives  49.8 us (26%)
  starting transfers between devices  20 us (10%)
  between operations  14.2 us (7%)
  local copies, waits for them, and re-layouts  4.67 us (2%)
  other arithmetic  2.95 us (2%)
  matrix products  2.56 us (1%)
    psum x1, waiting for transfers between devices, body(): sums = lax.psum(parts, 'col')  72 us
    all_to_all x1, blocking collectives, body(): got = lax.all_to_all(send, 'row', 0, 0, tiled=True)  49.8 us
    all_to_all x1, waiting for transfers between devices, body(): back = lax.all_to_all(back, 'row', 0, 0, tiled=True)  24.5 us
    all_to_all x1, starting transfers between devices, body(): back = lax.all_to_all(back, 'row', 0, 0, tiled=True)  20 us
  transfers between devices with their start and end apart: 2, of which 2 were waited for; matrix products, arithmetic and copies ran while one was open for 1% of the time, Pallas kernels for 0%

profile of v1, /device:TPU:2, one launch (start us, length us, event | category | flops | bytes accessed | tf_op | source)
XLA Modules:
  0.0 190.7 jit_solution(16417970009478469151)
XLA Ops:
  7.2 0.0 copy-start
  7.2 0.0 copy-start.4
  7.2 0.0 all-reduce.2.cloned.1.call-start
  7.2 0.7 fusion.34
  7.9 0.0 copy-done.4
  7.9 0.0 copy-start.1
  8.0 0.7 copy-done.1
  8.6 0.0 copy-start.2
  8.6 0.7 gather_fusion
  9.4 0.0 copy-done.2
  9.4 0.7 gather_fusion.1
  10.1 0.2 maximum_bitcast_fusion
  10.3 0.1 copy.22
  10.4 49.8 %all_to_all.18 = bf16[128,4,128]{2,1,0:T(4,128)(2,1)S(1)} all-to-all(bf16[128,4,128]{2,1,0:T(4,128)(2,1)S(1)} %copy.22), channel_id=1, replica_groups=mesh['row'=128,'col'=8] {'row'}, dimensions={0} | all-to-all | bytes 262144 | tf_op jit(solution)/shard_map/all_to_all | solution.py:29
  60.3 0.1 copy.24
  60.4 0.0 copy-start.3
  60.4 0.1 copy.25
  60.5 0.7 copy-done.3
  61.2 0.2 convolution_bitcast_fusion.2
  61.3 0.0 copy-done
  61.3 0.1 convolution_bitcast_fusion.3
  61.5 0.7 pad_maximum_fusion
  62.2 0.0 all-reduce.2.cloned.1.call-update
  62.2 72.0 %all-reduce.2.cloned.1.call-done = f32[2,256,128]{2,1,0:T(8,128)} async-done(((f32[2,256,128]{2,1,0:T(8,128)}), f32[2,256,128]{2,1,0:T(8,128)}) %all-reduce.2.cloned.1.call-update) | async-done | bytes 262160 | tf_op jit(solution)/shard_map/psum | solution.py:42
  134.2 1.3 fusion.4
  135.5 0.2 convolution_bitcast_fusion
  135.7 0.1 convolution_bitcast_fusion.1
  135.9 0.9 copy.26
  136.8 20.0 %all-to-all-start.1 = ((f32[128,4,128]{2,1,0:T(4,128)}), f32[128,4,128]{2,1,0:T(4,128)S(1)}, u32[]{:S(2)}, u32[]{:S(2)}) async-start(f32[128,4,128]{2,1,0:T(4,128)} %bitcast.21), calls=%async_computation.1 | async-start | bytes 524288 | tf_op jit(solution)/shard_map/all_to_all | solution.py:52
  156.7 0.8 convolution_bitcast_fusion.4
  157.6 0.8 convolution_bitcast_fusion.5
  158.4 24.5 %all-to-all-done.1 = f32[128,4,128]{2,1,0:T(4,128)S(1)} async-done(((f32[128,4,128]{2,1,0:T(4,128)}), f32[128,4,128]{2,1,0:T(4,128)S(1)}, u32[]{:S(2)}, u32[]{:S(2)}) %all-to-all-start.1) | async-done | bytes 262176 | tf_op jit(solution)/shard_map/all_to_all | solution.py:52
  182.9 0.2 fusion
  183.1 0.2 fusion.1
  183.2 0.6 copy_bitcast_fusion
  (8 shorter events, 0.1 us)
Async XLA Ops:
  7.2 54.2 %copy-start = (bf16[1,1,128,128]{3,2,1,0:T(8,128)(2,1)S(1)}, bf16[1,1,128,128]{3,2,1,0:T(8,128)(2,1)}, u32[]{:S(2)}) copy-start(bf16[1,1,128,128]{3,2,1,0:T(8,128)(2,1)} %param.8) | copy-start | bytes 98308
  7.2 0.7 copy-start.4
  7.2 127.0 %all-reduce.2.cloned.1.call-start = ((), (), s32[]{:S(2)}) async-start(), calls=%async_computation.2 | async-start | bytes 524288 | tf_op jit(solution)/shard_map/psum | solution.py:42
  7.9 0.7 copy-start.1
  8.6 0.7 copy-start.2
  60.4 0.8 copy-start.3
  136.8 46.1 %all-to-all-start.1 = ((f32[128,4,128]{2,1,0:T(4,128)}), f32[128,4,128]{2,1,0:T(4,128)S(1)}, u32[]{:S(2)}, u32[]{:S(2)}) async-start(f32[128,4,128]{2,1,0:T(4,128)} %bitcast.21), calls=%async_computation.1 | async-start | bytes 524288 | tf_op jit(solution)/shard_map/all_to_all | solution.py:52
Sparse Core Ops, SparseCore 0:
  62.4 71.7 all-reduce.1
